TPU v7x, 128 devices: a whole 4x4x4 slice. The times are simulated.
128 devices in a mesh: row: 8 (over z_hi, y), col: 16 (over z_lo, x, core).
Axes of the slice: x: 4, y: 4, z: 4 (z_hi: 2, z_lo: 2; z = z_hi * 2 + z_lo), core: 2. Of those that a mesh axis runs over, the one named last changes fastest.
Arguments:
- node_coords: float32 [3, 131072], P(None, ('row', 'col')), may hold values from -0.08 to 66.08, as said below
- tet_nodes: int32 [4, 864000], P(None, ('row', 'col')), may hold values from -1 to 1535, as said below
- bnd_nodes: int32 [55808], P(('row', 'col')), may hold values from -1 to 1023, as said below
- reaction: float32 [131072], P(('row', 'col')), may hold values from 0.05 to 0.5
- load: float32 [131072], P(('row', 'col')), may hold values from -8 to 8
- area_normal: float32 [3, 55808], P(None, ('row', 'col')), may hold values from -2 to 2
Outputs:
- solution: float32 [131072], P(('row', 'col'))
- demag_potential: float32 [55808], P(('row', 'col'))
Inputs may be any that keep to these rules, and one draw needn't show every extreme that they name: `tet_nodes`: own node n of a partition lies in its layer n // 256; layers run along the grain, partitions of a grain follow their col index. Each column lists the corners of one tetrahedron as indices into the partition's ghost-extended list (see the steps); each lattice cell of a grain is split into six tetrahedra around one of its main diagonals, the same on every partition that lists them; every tetrahedron of the grain that has an own node of the partition as a corner stands exactly once on that partition; -1 marks an empty column, all four entries then -1. Tetrahedra have volumes bounded away from zero. `bnd_nodes`: each own node on the surface of its grain stands in exactly one slot of its partition; other slots hold -1. The partitions at the two ends of a grain fill all 436 slots. `node_coords`: node positions of the grains' meshes.
All inputs are finite; a program needn't handle non-finite values.
Results may differ from a plain program's by a relative error of at most 0.0003.
Values sent between devices are 32-bit elements; how exact they have to be, the bound alone decides.
A program may use at most 128 MiB of HBM per device.

v0:
```python
import math
import jax
import jax.numpy as jnp
from jax import lax
from jax.sharding import PartitionSpec as P

QS = 16
ITERS = 3


def extended_2(x, sides, width):
    for axis, dim in sides:
        devices, length = (lax.axis_size(axis), x.shape[dim])
        up = [(i, (i + 1) % devices) for i in range(devices - 1)]
        down = [(j, i) for i, j in up]
        last = lax.slice_in_dim(x, length - width, length, axis=dim)
        leading = lax.slice_in_dim(x, 0, width, axis=dim)
        before = lax.ppermute(last, axis, up)
        after = lax.ppermute(leading, axis, down)
        x = jnp.concatenate([before, x, after], axis=dim)
    return x


def cross_product(left_vec, right_vec):
    return jnp.stack(
        [
            left_vec[1] * right_vec[2] - left_vec[2] * right_vec[1],
            left_vec[2] * right_vec[0] - left_vec[0] * right_vec[2],
            left_vec[0] * right_vec[1] - left_vec[1] * right_vec[0],
        ]
    )


def element_matrices(ext_coords, corners):
    present = corners[0] >= 0
    corner_ids = jnp.maximum(corners, 0)
    vertex_zero = ext_coords[:, corner_ids[0]]
    edge_one = ext_coords[:, corner_ids[1]] - vertex_zero
    edge_two = ext_coords[:, corner_ids[2]] - vertex_zero
    edge_three = ext_coords[:, corner_ids[3]] - vertex_zero
    normal_one = cross_product(edge_two, edge_three)
    normal_two = cross_product(edge_three, edge_one)
    normal_three = cross_product(edge_one, edge_two)
    normal_zero = -(normal_one + normal_two + normal_three)
    volume_six = jnp.sum(edge_one * normal_one, axis=0)
    safe_volume = jnp.abs(jnp.where(present, volume_six, 1.0))
    weights = jnp.where(present, 1.0 / (6.0 * safe_volume), 0.0)
    normals = jnp.stack([normal_zero, normal_one, normal_two, normal_three])
    stiffness = jnp.sum(normals[:, None] * normals[None, :], axis=2) * weights
    return (stiffness, corner_ids)


def assemble(values, corner_ids, ext_len, own_count):
    accumulated = (
        jnp.zeros((ext_len,), values.dtype).at[corner_ids.reshape(-1)].add(values.reshape(-1))
    )
    margin = (ext_len - own_count) // 2
    return accumulated[margin : margin + own_count]


def tile_sum(targets, sources):
    delta_x = targets[0][:, None] - sources[0][None, :]
    delta_y = targets[1][:, None] - sources[1][None, :]
    delta_z = targets[2][:, None] - sources[2][None, :]
    distance = delta_x * delta_x + delta_y * delta_y + delta_z * delta_z + 0.25
    numerator = (
        delta_x * sources[3][None, :]
        + delta_y * sources[4][None, :]
        + delta_z * sources[5][None, :]
    )
    inverse = lax.rsqrt(distance)
    return jnp.sum(numerator * inverse * inverse * inverse, axis=1) * (0.25 / math.pi)


def blocked_sum(targets, sources, width):
    columns = sources.shape[1]
    blocks = sources.reshape(6, columns // width, width).transpose(1, 0, 2)

    def scan_step(running, src_block):
        return (running + tile_sum(targets, src_block), None)

    running, unused = lax.scan(scan_step, jnp.zeros((targets.shape[1],), jnp.float32), blocks)
    return running


def local(node_coords, tet_nodes, bnd_nodes, reaction, load, area_normal):
    square = QS * QS
    own_count = load.shape[0]
    ext_len = own_count + 2 * square
    ext_coords = extended_2(node_coords, (("col", 1),), square)
    stiffness, corner_ids = element_matrices(ext_coords, tet_nodes)
    diag_terms = jnp.stack([stiffness[k, k] for k in range(4)])
    diagonal = reaction + assemble(diag_terms, corner_ids, ext_len, own_count)
    solution = jnp.zeros_like(load)
    residual = load
    precond = residual / diagonal
    direction = precond
    rz_now = lax.psum(jnp.sum(residual * precond), ("row", "col"))
    for iteration in range(ITERS):
        extended = extended_2(direction, (("col", 0),), square)
        products = jnp.sum(stiffness * extended[corner_ids][None], axis=1)
        image = reaction * direction + assemble(products, corner_ids, ext_len, own_count)
        curvature = lax.psum(jnp.sum(direction * image), ("row", "col"))
        step_size = rz_now / curvature
        solution = solution + step_size * direction
        residual = residual - step_size * image
        if iteration + 1 < ITERS:
            precond = residual / diagonal
            rz_next = lax.psum(jnp.sum(residual * precond), ("row", "col"))
            direction = precond + rz_next / rz_now * direction
            rz_now = rz_next
    slot_count = bnd_nodes.shape[0]
    live_mask = (bnd_nodes >= 0).astype(jnp.float32)
    slot_ids = jnp.maximum(bnd_nodes, 0)
    positions = node_coords[:, slot_ids] * live_mask[None, :]
    traces = solution[slot_ids] * live_mask
    weighted = area_normal * traces[None, :]
    sources = jnp.concatenate([positions, weighted], axis=0)
    row_sums = blocked_sum(
        positions, lax.all_gather(sources, ("row", "col"), axis=1, tiled=True), 8 * slot_count
    )
    demag_potential = live_mask * (-0.5 * traces + row_sums)
    return (solution, demag_potential)


def solution(mesh):
    placed = (
        P(None, ("row", "col")),
        P(None, ("row", "col")),
        P(("row", "col")),
        P(("row", "col")),
        P(("row", "col")),
        P(None, ("row", "col")),
    )
    return jax.shard_map(
        local,
        mesh=mesh,
        in_specs=placed,
        out_specs=(P(("row", "col")), P(("row", "col"))),
        check_vma=False,
    )
```

profile of v0, /device:TPU:1, one launch (start us, length us, event | category | flops | bytes accessed | tf_op | source)
XLA Modules:
  0.0 1903.4 jit_solution(17606528600907032549)
XLA Ops:
  18.4 13.5 gather_fusion.1
  31.9 13.5 gather_fusion
  45.4 13.4 gather_fusion.2
  58.9 13.5 gather_fusion.3
  83.0 10.5 multiply_reduce_fusion
  93.5 11.1 multiply_subtract_fusion.5
  123.2 9.2 fusion.14
  132.4 10.1 pad_maximum_fusion
  142.5 7.9 copy.129
  150.5 8.0 copy.130
  159.3 150.8 %scatter_custom_fusion = f32[1536]{0:T(1024)S(1)} fusion(s32[27000]{0:T(1024)S(1)} %fusion.15, f32[27000]{0:T(1024)S(1)} %reshape.409, f32[]{:T(128)} %constant.18.clone.1), kind=kCustom, calls=%fused_computation.122 | custom fusion | flops 27000 | bytes 6148 | tf_op jit(solution)/shard_map/scatter-add | solution.py:55
  318.8 138.7 %gather_fusion.4 = f32[27000]{0:T(1024)S(1)} fusion(f32[1536]{0:T(1024)S(1)} %pad_maximum_fusion.4, s32[27648]{0:T(1024)S(1)} %pad_clamp_fusion), kind=kCustom, calls=%fused_computation.4 | custom fusion | bytes 324000 | tf_op jit(solution)/shard_map/gather | solution.py:101
  458.2 150.8 %scatter_custom_fusion.1 = f32[1536]{0:T(1024)S(1)} fusion(s32[27000]{0:T(1024)S(1)} %fusion.15, f32[27000]{0:T(1024)S(1)} %reshape.417, f32[]{:T(128)} %constant.18.clone.1), kind=kCustom, calls=%fused_computation.120 | custom fusion | flops 27000 | bytes 6148 | tf_op jit(solution)/shard_map/scatter-add | solution.py:55
  609.6 104.3 %all-reduce = (f32[]{:T(128)}, f32[]{:T(128)}) all-reduce(f32[]{:T(128)} %get-tuple-element.75, f32[]{:T(128)} %get-tuple-element.74), channel_id=1, replica_groups=mesh['row'=8,'col'=16] {'row','col'}, use_global_device_ids=true, to_apply=%region_4.5 | all-reduce | flops 2 | bytes 16 | tf_op jit(solution)/shard_map/psum | solution.py:98
  715.8 62.6 %psum.44 = f32[]{:T(128)} all-reduce(f32[]{:T(128)} %get-tuple-element.88), channel_id=1, replica_groups=mesh['row'=8,'col'=16] {'row','col'}, use_global_device_ids=true, to_apply=%region_10.11 | all-reduce | flops 1 | bytes 8 | tf_op jit(solution)/shard_map/psum | solution.py:109
  788.3 138.6 %gather_fusion.5 = f32[27000]{0:T(1024)S(1)} fusion(f32[1536]{0:T(1024)S(1)} %pad_maximum_fusion.5, s32[27648]{0:T(1024)S(1)} %pad_clamp_fusion), kind=kCustom, calls=%fused_computation.5 | custom fusion | bytes 324000 | tf_op jit(solution)/shard_map/gather | solution.py:101
  927.5 150.8 %scatter_custom_fusion.2 = f32[1536]{0:T(1024)S(1)} fusion(s32[27000]{0:T(1024)S(1)} %fusion.15, f32[27000]{0:T(1024)S(1)} %reshape.425, f32[]{:T(128)} %constant.18.clone.1), kind=kCustom, calls=%fused_computation.118 | custom fusion | flops 27000 | bytes 6148 | tf_op jit(solution)/shard_map/scatter-add | solution.py:55
  1078.8 80.1 %psum.45 = f32[]{:T(128)} all-reduce(f32[]{:T(128)} %multiply_reduce_fusion.6), channel_id=1, replica_groups=mesh['row'=8,'col'=16] {'row','col'}, use_global_device_ids=true, to_apply=%region_14.15 | all-reduce | flops 1 | bytes 8 | tf_op jit(solution)/shard_map/psum | solution.py:103
  1160.9 63.5 %psum.46 = f32[]{:T(128)} all-reduce(f32[]{:T(128)} %multiply_reduce_fusion.5), channel_id=1, replica_groups=mesh['row'=8,'col'=16] {'row','col'}, use_global_device_ids=true, to_apply=%region_16.17 | all-reduce | flops 1 | bytes 8 | tf_op jit(solution)/shard_map/psum | solution.py:109
  1233.0 138.6 %gather_fusion.6 = f32[27000]{0:T(1024)S(1)} fusion(f32[1536]{0:T(1024)S(1)} %pad_maximum_fusion.6, s32[27648]{0:T(1024)S(1)} %pad_clamp_fusion), kind=kCustom, calls=%fused_computation.6 | custom fusion | bytes 324000 | tf_op jit(solution)/shard_map/gather | solution.py:101
  1372.1 150.8 %scatter_custom_fusion.3 = f32[1536]{0:T(1024)S(1)} fusion(s32[27000]{0:T(1024)S(1)} %fusion.15, f32[27000]{0:T(1024)S(1)} %reshape.433, f32[]{:T(128)} %constant.18.clone.1), kind=kCustom, calls=%fused_computation.116 | custom fusion | flops 27000 | bytes 6148 | tf_op jit(solution)/shard_map/scatter-add | solution.py:55
  1524.9 81.0 %psum.47 = f32[]{:T(128)} all-reduce(f32[]{:T(128)} %fusion.21), channel_id=1, replica_groups=mesh['row'=8,'col'=16] {'row','col'}, use_global_device_ids=true, to_apply=%region_20.21 | all-reduce | flops 1 | bytes 8 | tf_op jit(solution)/shard_map/psum | solution.py:103
  1610.3 191.4 %all-gather.3.cloned.1.call-done = f32[128,436,6]{1,2,0:T(8,128)} async-done(((f32[1,436,6]{1,2,0:T(8,128)}), f32[128,436,6]{1,2,0:T(8,128)}) %all-gather.3.cloned.1.call-update) | async-done | bytes 1339408 | tf_op jit(solution)/shard_map/all_gather | solution.py:120
  1806.3 89.4 %while.11 = (s32[]{:T(128)}, f32[436]{0:T(512)S(1)}, f32[3,436]{1,0:T(4,128)S(1)}, f32[16,6,3488]{2,0,1:T(8,128)S(1)}, s32[]{:T(128)}, /*index=5*/s32[]{:T(128)}, s32[]{}, s32[]{}, s32[]{}, s32[]{}, /*index=10*/s32[]{}) while((s32[]{:T(128)}, f32[436]{0:T(512)S(1)}, f32[3,436]{1,0:T(4,128)S(1)}, f32[16,6,3488]{2,0,1:T(8,128)S(1)}, ...), condition=%wide.region_23.24_spmd.clone, body=%wide.region_21.23_spmd.clone.sunk | while | flops 27374704 | bytes 274011 | solution.py:82
  (173 shorter events, 168.6 us)
Async XLA Ops:
  7.2 1794.5 %all-gather.3.cloned.1.call-start = ((), (), s32[]{:S(2)}) async-start(), calls=%async_computation | async-start | bytes 2113536 | tf_op jit(solution)/shard_map/all_gather | solution.py:120
  7.9 9.4 collective-permute-start
  12.4 4.9 collective-permute-start.1
  77.0 6.1 copy-start.1
  93.5 11.1 copy-start.2
  104.7 6.6 copy-start.6
  111.3 3.6 copy-start.8
  115.0 7.2 copy-start.3
  115.0 7.2 copy-start.4
  115.0 7.2 copy-start.5
  115.0 8.3 copy-start.7
  150.5 159.6 %copy-start.9 = (f32[1024]{0:T(1024)S(1)}, f32[1024]{0:T(1024)}, u32[]{:S(2)}) copy-start(f32[1024]{0:T(1024)} %param.11) | copy-start | bytes 12292
  150.5 159.6 %copy-start.11 = (f32[1024]{0:T(1024)S(1)}, f32[1024]{0:T(1024)}, u32[]{:S(2)}) copy-start(f32[1024]{0:T(1024)} %param.12) | copy-start | bytes 12292
  310.1 5.8 collective-permute-start.2
  313.9 4.9 collective-permute-start.3
  779.8 5.5 collective-permute-start.4
  783.4 4.9 collective-permute-start.5
  788.3 372.6 %copy-start.13 = (s32[436]{0:T(512)S(1)}, s32[436]{0:T(512)}, u32[]{:S(2)}) copy-start(s32[436]{0:T(512)} %param.10) | copy-start | bytes 5236
  788.3 441.9 %copy-start.10 = (f32[3,1024]{1,0:T(4,128)S(1)}, f32[3,1024]{1,0:T(4,128)}, u32[]{:S(2)}) copy-start(f32[3,1024]{1,0:T(4,128)} %param.8) | copy-start | bytes 36868
  1225.8 4.6 collective-permute-start.6
  1228.1 4.9 collective-permute-start.7
  1371.5 238.1 %copy-start.12 = (f32[3,436]{1,0:T(4,128)S(1)}, f32[3,436]{1,0:T(4,128)}, u32[]{:S(2)}) copy-start(f32[3,436]{1,0:T(4,128)} %param.13) | copy-start | bytes 15700
  1607.2 198.2 %copy-start = (f32[1024]{0:T(1024)}, f32[1024]{0:T(1024)S(1)}, u32[]{:S(2)}) copy-start(f32[1024]{0:T(1024)S(1)} %multiply_add_fusion) | copy-start | bytes 12292
Sparse Core Ops, SparseCore 0:
  1610.4 191.2 all-gather.2
where the time goes:
time: 1910 us; the launch traced here: 1900 us
  other arithmetic  766 us (40%)
  local copies, waits for them, and re-layouts  502 us (26%)
  blocking collectives  392 us (21%)
  waiting for transfers between devices  200 us (10%)
  starting transfers between devices  22.1 us (1%)
  between operations  21.6 us (1%)
    scatter-add x4, other arithmetic, assemble(): jnp.zeros((ext_len,), values.dtype).at[corner_ids.reshape(-1)]  603 us
    gather x6, local copies, waits for them, and re-layouts, local(): products = jnp.sum(stiffness * extended[corner_ids][None], axis=1)  416 us
    all_gather x1, waiting for transfers between devices, local(): lax.all_gather(sources, ('row', 'col'), axis=1, tiled=True)  191 us
    psum x2, blocking collectives, local(): curvature = lax.psum(jnp.sum(direction * image), ('row', 'col'))  161 us
    psum x2, blocking collectives, local(): rz_next = lax.psum(jnp.sum(residual * precond), ('row', 'col'))  126 us
    psum x1, blocking collectives, local(): rz_now = lax.psum(jnp.sum(residual * precond), ('row', 'col'))  104 us
    reduce_sum x16, other arithmetic, tile_sum(): jnp.sum(numerator * inverse * inverse * inverse, axis=1) * (0.25 / math.pi)  84.6 us
  transfers between devices with their start and end apart: 9, of which 4 were waited for; matrix products, arithmetic and copies ran while one was open for 0% of the time, Pallas kernels for 0%

commit v1 on v0

--- a/solution.py
+++ b/solution.py
@@ -117,7 +117,17 @@
     weighted = area_normal * traces[None, :]
     sources = jnp.concatenate([positions, weighted], axis=0)
     row_sums = blocked_sum(
-        positions, lax.all_gather(sources, ("row", "col"), axis=1, tiled=True), 8 * slot_count
+        positions,
+        jnp.concatenate(
+            lax.all_to_all(
+                jnp.stack([sources for _ in range(lax.axis_size(("row", "col")))]),
+                ("row", "col"),
+                0,
+                0,
+            ),
+            axis=1,
+        ),
+        8 * slot_count,
     )
     demag_potential = live_mask * (-0.5 * traces + row_sums)
     return (solution, demag_potential)

time: 1910 us -> 1750 us (0.916)
  waiting for transfers between devices: 200 us -> 39.2 us
    all_gather x1 -> x0, waiting for transfers between devices: 191 us -> none  [local(): lax.all_gather(sources, ('row', 'col'), axis=1, tiled=True)]
    all_to_all x0 -> x1, waiting for transfers between devices: none -> 30.7 us  [local(): lax.all_to_all(jnp.stack([sources for _ in range(lax.axis_size(('row', 'c...]
where the time goes in v1:
time: 1750 us; the launch traced here: 1740 us
  other arithmetic  766 us (44%)
  local copies, waits for them, and re-layouts  503 us (29%)
  blocking collectives  392 us (22%)
  waiting for transfers between devices  39.2 us (2%)
  starting transfers between devices  27.6 us (2%)
    scatter-add x4, other arithmetic, assemble(): jnp.zeros((ext_len,), values.dtype).at[corner_ids.reshape(-1)]  603 us
    gather x6, local copies, waits for them, and re-layouts, local(): products = jnp.sum(stiffness * extended[corner_ids][None], axis=1)  416 us
    psum x2, blocking collectives, local(): curvature = lax.psum(jnp.sum(direction * image), ('row', 'col'))  161 us
    psum x2, blocking collectives, local(): rz_next = lax.psum(jnp.sum(residual * precond), ('row', 'col'))  126 us
    psum x1, blocking collectives, local(): rz_now = lax.psum(jnp.sum(residual * precond), ('row', 'col'))  104 us
    reduce_sum x16, other arithmetic, tile_sum(): jnp.sum(numerator * inverse * inverse * inverse, axis=1) * (0.25 / math.pi)  84.6 us
  transfers between devices with their start and end apart: 9, of which 4 were waited for; matrix products, arithmetic and copies ran while one was open for 0% of the time, Pallas kernels for 0%

profile of v1, /device:TPU:1, one launch (start us, length us, event | category | flops | bytes accessed | tf_op | source)
XLA Modules:
  0.0 1735.6 jit_solution(16594313370624064833)
XLA Ops:
  11.8 13.5 gather_fusion.1
  25.3 13.5 gather_fusion
  38.8 13.4 gather_fusion.2
  52.3 13.5 gather_fusion.3
  76.4 10.5 multiply_reduce_fusion
  87.0 11.1 multiply_subtract_fusion.5
  116.7 9.2 fusion.14
  125.9 10.1 pad_maximum_fusion
  135.9 7.9 copy.130
  143.9 8.0 copy.131
  152.7 150.8 %scatter_custom_fusion = f32[1536]{0:T(1024)S(1)} fusion(s32[27000]{0:T(1024)S(1)} %fusion.15, f32[27000]{0:T(1024)S(1)} %reshape.411, f32[]{:T(128)} %constant.18.clone.1), kind=kCustom, calls=%fused_computation.122 | custom fusion | flops 27000 | bytes 6148 | tf_op jit(solution)/shard_map/scatter-add | solution.py:55
  312.3 138.7 %gather_fusion.4 = f32[27000]{0:T(1024)S(1)} fusion(f32[1536]{0:T(1024)S(1)} %pad_maximum_fusion.5, s32[27648]{0:T(1024)S(1)} %pad_clamp_fusion), kind=kCustom, calls=%fused_computation.4 | custom fusion | bytes 324000 | tf_op jit(solution)/shard_map/gather | solution.py:101
  451.6 150.8 %scatter_custom_fusion.1 = f32[1536]{0:T(1024)S(1)} fusion(s32[27000]{0:T(1024)S(1)} %fusion.15, f32[27000]{0:T(1024)S(1)} %reshape.419, f32[]{:T(128)} %constant.18.clone.1), kind=kCustom, calls=%fused_computation.120 | custom fusion | flops 27000 | bytes 6148 | tf_op jit(solution)/shard_map/scatter-add | solution.py:55
  603.0 104.3 %all-reduce = (f32[]{:T(128)}, f32[]{:T(128)}) all-reduce(f32[]{:T(128)} %get-tuple-element.75, f32[]{:T(128)} %get-tuple-element.74), channel_id=1, replica_groups=mesh['row'=8,'col'=16] {'row','col'}, use_global_device_ids=true, to_apply=%region_4.5 | all-reduce | flops 2 | bytes 16 | tf_op jit(solution)/shard_map/psum | solution.py:98
  709.3 62.6 %psum.44 = f32[]{:T(128)} all-reduce(f32[]{:T(128)} %get-tuple-element.88), channel_id=1, replica_groups=mesh['row'=8,'col'=16] {'row','col'}, use_global_device_ids=true, to_apply=%region_10.11 | all-reduce | flops 1 | bytes 8 | tf_op jit(solution)/shard_map/psum | solution.py:109
  781.7 138.6 %gather_fusion.5 = f32[27000]{0:T(1024)S(1)} fusion(f32[1536]{0:T(1024)S(1)} %pad_maximum_fusion.6, s32[27648]{0:T(1024)S(1)} %pad_clamp_fusion), kind=kCustom, calls=%fused_computation.5 | custom fusion | bytes 324000 | tf_op jit(solution)/shard_map/gather | solution.py:101
  920.9 150.8 %scatter_custom_fusion.2 = f32[1536]{0:T(1024)S(1)} fusion(s32[27000]{0:T(1024)S(1)} %fusion.15, f32[27000]{0:T(1024)S(1)} %reshape.427, f32[]{:T(128)} %constant.18.clone.1), kind=kCustom, calls=%fused_computation.118 | custom fusion | flops 27000 | bytes 6148 | tf_op jit(solution)/shard_map/scatter-add | solution.py:55
  1072.3 80.1 %psum.45 = f32[]{:T(128)} all-reduce(f32[]{:T(128)} %multiply_reduce_fusion.6), channel_id=1, replica_groups=mesh['row'=8,'col'=16] {'row','col'}, use_global_device_ids=true, to_apply=%region_14.15 | all-reduce | flops 1 | bytes 8 | tf_op jit(solution)/shard_map/psum | solution.py:103
  1154.3 63.5 %psum.46 = f32[]{:T(128)} all-reduce(f32[]{:T(128)} %multiply_reduce_fusion.5), channel_id=1, replica_groups=mesh['row'=8,'col'=16] {'row','col'}, use_global_device_ids=true, to_apply=%region_16.17 | all-reduce | flops 1 | bytes 8 | tf_op jit(solution)/shard_map/psum | solution.py:109
  1226.4 138.6 %gather_fusion.6 = f32[27000]{0:T(1024)S(1)} fusion(f32[1536]{0:T(1024)S(1)} %pad_maximum_fusion.7, s32[27648]{0:T(1024)S(1)} %pad_clamp_fusion), kind=kCustom, calls=%fused_computation.6 | custom fusion | bytes 324000 | tf_op jit(solution)/shard_map/gather | solution.py:101
  1365.6 150.8 %scatter_custom_fusion.3 = f32[1536]{0:T(1024)S(1)} fusion(s32[27000]{0:T(1024)S(1)} %fusion.15, f32[27000]{0:T(1024)S(1)} %reshape.435, f32[]{:T(128)} %constant.18.clone.1), kind=kCustom, calls=%fused_computation.116 | custom fusion | flops 27000 | bytes 6148 | tf_op jit(solution)/shard_map/scatter-add | solution.py:55
  1518.3 81.0 %psum.47 = f32[]{:T(128)} all-reduce(f32[]{:T(128)} %fusion.21), channel_id=1, replica_groups=mesh['row'=8,'col'=16] {'row','col'}, use_global_device_ids=true, to_apply=%region_20.21 | all-reduce | flops 1 | bytes 8 | tf_op jit(solution)/shard_map/psum | solution.py:103
  1610.3 30.7 %all-to-all-done = f32[128,6,436]{2,1,0:T(8,128)S(1)} async-done(((f32[128,6,436]{2,1,0:T(8,128)}), f32[128,6,436]{2,1,0:T(8,128)S(1)}, u32[]{:S(2)}, u32[]{:S(2)}) %all-to-all-start) | async-done | bytes 1339424 | tf_op jit(solution)/shard_map/all_to_all | solution.py:122
  1645.4 89.4 %while.11 = (s32[]{:T(128)}, f32[436]{0:T(512)S(1)}, f32[3,436]{1,0:T(4,128)S(1)}, f32[16,6,3488]{2,0,1:T(8,128)S(1)}, s32[]{:T(128)}, /*index=5*/s32[]{:T(128)}, s32[]{}, s32[]{}, s32[]{}, s32[]{}, /*index=10*/s32[]{}) while((s32[]{:T(128)}, f32[436]{0:T(512)S(1)}, f32[3,436]{1,0:T(4,128)S(1)}, f32[16,6,3488]{2,0,1:T(8,128)S(1)}, ...), condition=%wide.region_23.24_spmd.clone, body=%wide.region_21.23_spmd.clone.sunk | while | flops 27374704 | bytes 274011 | solution.py:82
  (172 shorter events, 174.9 us)
Async XLA Ops:
  1.3 9.4 collective-permute-start
  5.8 4.9 collective-permute-start.1
  70.4 6.1 copy-start.1
  87.0 11.1 copy-start.2
  98.1 6.6 copy-start.6
  104.8 3.6 copy-start.8
  108.4 7.2 copy-start.3
  108.4 7.2 copy-start.4
  108.4 7.2 copy-start.5
  108.4 8.3 copy-start.7
  143.9 159.6 %copy-start.9 = (f32[1024]{0:T(1024)S(1)}, f32[1024]{0:T(1024)}, u32[]{:S(2)}) copy-start(f32[1024]{0:T(1024)} %param.11) | copy-start | bytes 12292
  143.9 159.6 %copy-start.11 = (f32[1024]{0:T(1024)S(1)}, f32[1024]{0:T(1024)}, u32[]{:S(2)}) copy-start(f32[1024]{0:T(1024)} %param.12) | copy-start | bytes 12292
  303.5 5.8 collective-permute-start.2
  307.4 4.9 collective-permute-start.3
  773.2 5.5 collective-permute-start.4
  776.8 4.9 collective-permute-start.5
  781.7 372.6 %copy-start.13 = (s32[436]{0:T(512)S(1)}, s32[436]{0:T(512)}, u32[]{:S(2)}) copy-start(s32[436]{0:T(512)} %param.10) | copy-start | bytes 5236
  781.7 441.9 %copy-start.10 = (f32[3,1024]{1,0:T(4,128)S(1)}, f32[3,1024]{1,0:T(4,128)}, u32[]{:S(2)}) copy-start(f32[3,1024]{1,0:T(4,128)} %param.8) | copy-start | bytes 36868
  1219.2 4.6 collective-permute-start.6
  1221.5 4.9 collective-permute-start.7
  1365.0 238.1 %copy-start.12 = (f32[3,436]{1,0:T(4,128)S(1)}, f32[3,436]{1,0:T(4,128)}, u32[]{:S(2)}) copy-start(f32[3,436]{1,0:T(4,128)} %param.13) | copy-start | bytes 15700
  1600.7 4.0 copy-start
  1604.7 36.3 %all-to-all-start = ((f32[128,6,436]{2,1,0:T(8,128)}), f32[128,6,436]{2,1,0:T(8,128)S(1)}, u32[]{:S(2)}, u32[]{:S(2)}) async-start(f32[128,6,436]{2,1,0:T(8,128)} %stack.62), calls=%async_computation | async-start | bytes 4194304 | tf_op jit(solution)/shard_map/all_to_all | solution.py:122
